TPU v7x, 32 devices: a whole 2x2x4 slice. The times are simulated.
32 devices in a mesh: grp: 2 (over y), cls: 8 (over z, x), img: 2 (over core).
Axes of the slice: x: 2, y: 2, z: 4, core: 2. Of those that a mesh axis runs over, the one named last changes fastest.
Arguments:
- embeddings: bfloat16 [4096, 1536], P(('grp', 'img'), 'cls'), parts along dimension 0, may hold values from -6 to 6, as said below
- labels: int32 [4096], P(('grp', 'img')), parts along dimension 0, may hold values from 0 to 1023
- weights: float32 [3072, 1024], P(('grp', 'img'), 'cls'), parts along dimension 0, may hold values from -12 to 12, as said below
- strength: int32 [2], P('grp'), parts along dimension 0, may hold values from 0 to 3
Outputs:
- new_weights: float32 [3072, 1024], P(('grp', 'img'), 'cls'), parts along dimension 0
- losses: float32 [4096], P(('grp', 'img')), parts along dimension 0
There are 2 independent parts, one for each index of `grp`. A program takes and returns all parts, laid end to end along the dimension named above; each array names one. Nothing has to cross between parts.
Inputs may be any that keep to these rules, and one draw needn't show every extreme that they name: embeddings of order one. Initial probe weights of order a few.
All inputs are finite; a program needn't handle non-finite values.
Results may differ from a plain program's by a relative error of at most 0.0032.
Values may be sent and summed in bfloat16 or wider, within the bound.
A program may use at most 64 MiB of HBM per device.

v0:
```python
import math
import jax
import jax.numpy as jnp
from jax import lax
from jax.sharding import PartitionSpec as P

D = 1536
ITERS = 2


def shrink(master, grad, lam):
    moved = master - 16.0 * grad
    return jnp.sign(moved) * jnp.maximum(jnp.abs(moved) - lam, 0.0)


def shards(embeddings, labels, weights, strength):
    scale = 1.0 / math.sqrt(D)
    lam = 16.0 * 0.01 * jnp.exp2(strength[0].astype(jnp.float32))
    full_x = lax.all_gather(embeddings, "cls", axis=1, tiled=True)
    cls_width = weights.shape[1]
    first_class = lax.axis_index("cls") * cls_width
    classes = first_class + lax.iota(jnp.int32, cls_width)
    onehot = (labels[:, None] == classes[None, :]).astype(jnp.float32)
    master = lax.all_gather(weights, "img", axis=0, tiled=True)
    operand = master.astype(jnp.bfloat16)
    losses = jnp.zeros((labels.shape[0],), jnp.float32)
    for step in range(ITERS):
        logits = jnp.dot(full_x, operand, preferred_element_type=jnp.float32) * scale
        local_top = jnp.max(logits, axis=1)
        label_term = jnp.sum(logits * onehot, axis=1)
        top = lax.pmax(local_top, "cls")
        total, picked = lax.psum(
            (jnp.sum(jnp.exp(logits - top[:, None]), axis=1), label_term), "cls"
        )
        lse = top + jnp.log(total)
        losses = lse - picked
        resid = (jnp.exp(logits - lse[:, None]) - onehot).astype(jnp.bfloat16)
        grad_local = (
            lax.dot_general(
                full_x, resid, (((0,), (0,)), ((), ())), preferred_element_type=jnp.float32
            )
            * scale
        )
        grad = lax.psum(grad_local, "img")
        master = shrink(master, grad, lam)
        operand = master.astype(jnp.bfloat16)
    rows = weights.shape[0]
    new_weights = lax.dynamic_slice_in_dim(master, lax.axis_index("img") * rows, rows, 0)
    return (new_weights, losses)


def solution(mesh):
    placed = (P(("grp", "img"), "cls"), P(("grp", "img")), P(("grp", "img"), "cls"), P("grp"))
    return jax.shard_map(
        shards,
        mesh=mesh,
        in_specs=placed,
        out_specs=(P(("grp", "img"), "cls"), P(("grp", "img"))),
        check_vma=False,
    )
```

profile of v0, /device:TPU:0, one launch (start us, length us, event | category | flops | bytes accessed | tf_op | source)
XLA Modules:
  0.0 210.3 jit_solution(16586278713644996422)
XLA Ops:
  7.2 0.0 all-gather.2.cloned.1.call-start
  7.2 0.7 all-gather.2.cloned.1.call-update
  7.9 0.0 all-reduce.4.cloned.1.call-start
  7.9 1.2 copy.6
  9.1 0.0 copy-start.2
  9.1 2.6 %all_gather.6 = f32[1536,128]{0,1:T(8,128)} all-gather(f32[768,128]{0,1:T(8,128)S(1)} %copy.6), channel_id=1, replica_groups=mesh['grp'=2,'cls'=8,'img'=2] {'img'}, dimensions={0}, use_global_device_ids=true | all-gather | bytes 1179648 | tf_op jit(solution)/shard_map/all_gather | solution.py:24
  11.7 61.6 %all-gather.2.cloned.1.call-done = bf16[1024,1536]{0,1:T(8,128)(2,1)} async-done(((bf16[1024,192]{0,1:T(8,128)(2,1)}), bf16[1024,1536]{0,1:T(8,128)(2,1)}) %all-gather.2.cloned.1.call-update) | async-done | bytes 3145744 | tf_op jit(solution)/shard_map/all_gather | solution.py:19
  73.4 0.0 copy-start
  73.4 3.7 %fusion.19 = (f32[1024]{0:T(1024)S(1)}, f32[1024,128]{0,1:T(8,128)}) fusion(bf16[1024,1536]{0,1:T(8,128)(2,1)} %all-gather.2.cloned.1.call-done, f32[1536,128]{0,1:T(8,128)} %all_gather.6), kind=kOutput, calls=%fused_computation.34 | convolution fusion | flops 403110912 | bytes 4460544 | tf_op jit(solution)/shard_map/dot_general | solution.py:28
  77.0 19.0 %pmax.14 = f32[1024]{0:T(1024)S(1)} all-reduce(f32[1024]{0:T(1024)S(1)} %get-tuple-element.10), channel_id=1, replica_groups=mesh['grp'=2,'cls'=8,'img'=2] {'cls'}, use_global_device_ids=true, to_apply=%region_1.0 | all-reduce | flops 1024 | bytes 8192 | tf_op jit(solution)/shard_map/pmax | solution.py:31
  96.1 1.1 exponential_reduce_fusion
  97.2 17.2 %psum.35 = f32[1024]{0:T(1024)S(1)} all-reduce(f32[1024]{0:T(1024)S(1)} %exponential_reduce_fusion), channel_id=1, replica_groups=mesh['grp'=2,'cls'=8,'img'=2] {'cls'}, use_global_device_ids=true, to_apply=%region_3.0 | all-reduce | flops 1024 | bytes 8192 | tf_op jit(solution)/shard_map/psum | solution.py:32
  114.4 0.0 copy-done.2
  114.4 0.0 copy-done
  114.4 3.1 %fusion = f32[1536,128]{0,1:T(8,128)} fusion(bf16[1024,1536]{0,1:T(8,128)(2,1)S(1)} %copy-done, f32[1024,128]{0,1:T(8,128)} %get-tuple-element.11, s32[1024]{0:T(1024)S(1)} %copy-done.2, f32[1024]{0:T(1024)S(1)} %log_add_fusion.1, s32[128]{0:T(128)S(1)} %iota_add_fusion), kind=kOutput, calls=%fused_computation.2 | convolution fusion | flops 403505152 | bytes 4465152 | tf_op jit(solution)/shard_map/dot_general | solution.py:39
  117.6 0.0 all-reduce.4.cloned.1.call-update
  117.6 0.0 all-reduce.6.cloned.1.call-start
  118.3 17.2 %all-reduce.4.cloned.1.call-done = f32[1536,128]{0,1:T(8,128)} async-done(((f32[1536,128]{0,1:T(8,128)}), f32[1536,128]{0,1:T(8,128)}) %all-reduce.4.cloned.1.call-update) | async-done | bytes 786448 | tf_op jit(solution)/shard_map/psum | solution.py:44
  135.6 1.7 maximum_multiply_fusion
  137.3 0.0 copy-start.1
  137.3 0.9 copy-done.1
  138.2 1.4 fusion.20
  139.5 21.6 %pmax.15 = f32[1024]{0:T(1024)S(1)} all-reduce(f32[1024]{0:T(1024)S(1)} %get-tuple-element.12), channel_id=1, replica_groups=mesh['grp'=2,'cls'=8,'img'=2] {'cls'}, use_global_device_ids=true, to_apply=%region_6.0 | all-reduce | flops 1024 | bytes 8192 | tf_op jit(solution)/shard_map/pmax | solution.py:31
  161.2 1.2 fusion.2
  162.3 17.4 %all-reduce = (f32[1024]{0:T(1024)S(1)}, f32[1024]{0:T(1024)S(1)}) all-reduce(f32[1024]{0:T(1024)S(1)} %get-tuple-element.5, f32[1024]{0:T(1024)S(1)} %get-tuple-element.4), channel_id=1, replica_groups=mesh['grp'=2,'cls'=8,'img'=2] {'cls'}, use_global_device_ids=true, to_apply=%region_8.0 | all-reduce | flops 2048 | bytes 16384 | tf_op jit(solution)/shard_map/psum | solution.py:32
  179.7 0.6 fusion.18
  180.3 3.1 %fusion.1 = f32[1536,128]{0,1:T(8,128)} fusion(bf16[1024,1536]{0,1:T(8,128)(2,1)S(1)} %copy-done, f32[128,1024]{1,0:T(8,128)} %get-tuple-element.13, f32[1024]{0:T(1024)S(1)} %get-tuple-element.9, s32[1024]{0:T(1024)S(1)} %copy-done.2, s32[128]{0:T(128)S(1)} %iota_add_fusion), kind=kOutput, calls=%fused_computation.3 | convolution fusion | flops 403505152 | bytes 4465152 | tf_op jit(solution)/shard_map/dot_general | solution.py:39
  183.5 0.0 all-reduce.6.cloned.1.call-update
  183.5 18.1 %all-reduce.6.cloned.1.call-done = f32[1536,128]{0,1:T(8,128)} async-done(((f32[1536,128]{0,1:T(8,128)}), f32[1536,128]{0,1:T(8,128)}) %all-reduce.6.cloned.1.call-update) | async-done | bytes 786448 | tf_op jit(solution)/shard_map/psum | solution.py:44
  201.5 1.3 maximum_multiply_fusion.1
  202.8 0.9 copy.7
  (2 shorter events, 0.0 us)
Async XLA Ops:
  7.2 66.2 %all-gather.2.cloned.1.call-start = ((), (), s32[]{:S(2)}) async-start(), calls=%async_computation | async-start | bytes 3538944 | tf_op jit(solution)/shard_map/all_gather | solution.py:19
  7.9 127.7 %all-reduce.4.cloned.1.call-start = ((), (), s32[]{:S(2)}) async-start(), calls=%async_computation.1 | async-start | bytes 1572864 | tf_op jit(solution)/shard_map/psum | solution.py:44
  9.1 105.3 %copy-start.2 = (s32[1024]{0:T(1024)S(1)}, s32[1024]{0:T(1024)}, u32[]{:S(2)}) copy-start(s32[1024]{0:T(1024)} %param.5) | copy-start | bytes 12292
  73.4 41.1 %copy-start = (bf16[1024,1536]{0,1:T(8,128)(2,1)S(1)}, bf16[1024,1536]{0,1:T(8,128)(2,1)}, u32[]{:S(2)}) copy-start(bf16[1024,1536]{0,1:T(8,128)(2,1)} %all-gather.2.cloned.1.call-done) | copy-start | bytes 9437188
  117.6 83.9 %all-reduce.6.cloned.1.call-start = ((), (), s32[]{:S(2)}) async-start(), calls=%async_computation.2 | async-start | bytes 1572864 | tf_op jit(solution)/shard_map/psum | solution.py:44
  137.3 0.9 copy-start.1
Sparse Core Ops, SparseCore 0:
  10.2 63.1 all-gather.1
  117.7 17.8 all-reduce.3
  183.6 17.8 all-reduce.5
where the time goes:
time: 211 us; the launch traced here: 210 us
  waiting for transfers between devices  97.6 us (46%)
  blocking collectives  77.8 us (37%)
  between operations  14.5 us (7%)
  matrix products  11.3 us (5%)
  other arithmetic  5.92 us (3%)
  local copies, waits for them, and re-layouts  2.95 us (1%)
    all_gather x1, waiting for transfers between devices, shards(): full_x = lax.all_gather(embeddings, 'cls', axis=1, tiled=True)  61.6 us
    pmax x2, blocking collectives, shards(): top = lax.pmax(local_top, 'cls')  40.6 us
    psum x2, waiting for transfers between devices, shards(): grad = lax.psum(grad_local, 'img')  35.3 us
    psum x2, blocking collectives, shards(): lax.psum((jnp.sum(jnp.exp(logits - top[:, None]), axis=1), label_term), '...  34.6 us
    dot_general x2, matrix products, shards(): lax.dot_general(full_x, resid, (((0,), (0,)), ((), ())), preferred_elemen...  6.27 us
    dot_general x2, matrix products, shards(): jnp.dot(full_x, operand, preferred_element_type=jnp.float32) * scale  5.05 us
  transfers between devices with their start and end apart: 3, of which 3 were waited for; matrix products, arithmetic and copies ran while one was open for 1% of the time, Pallas kernels for 0%

commit v1 on v0

--- a/solution.py
+++ b/solution.py
@@ -41,7 +41,7 @@
             )
             * scale
         )
-        grad = lax.psum(grad_local, "img")
+        grad = jnp.sum(lax.all_gather(grad_local, "img"), axis=0)
         master = shrink(master, grad, lam)
         operand = master.astype(jnp.bfloat16)
     rows = weights.shape[0]

time: 211 us -> 203 us (0.962)
  waiting for transfers between devices: 97.6 us -> 78.8 us
  local copies, waits for them, and re-layouts: 2.95 us -> 9.03 us
  other arithmetic: 5.92 us -> 10.8 us
    psum x2 -> x0, waiting for transfers between devices: 35.3 us -> none  [shards(): grad = lax.psum(grad_local, 'img')]
    all_gather x0 -> x2, waiting for transfers between devices: none -> 16.5 us  [shards(): grad = jnp.sum(lax.all_gather(grad_local, 'img'), axis=0)]
    all_gather x0 -> x2, local copies, waits for them, and re-layouts: none -> 6.07 us  [shards(): grad = jnp.sum(lax.all_gather(grad_local, 'img'), axis=0)]
    reduce_sum x0 -> x2, other arithmetic: none -> 6.02 us  [shards(): grad = jnp.sum(lax.all_gather(grad_local, 'img'), axis=0)]
where the time goes in v1:
time: 203 us; the launch traced here: 202 us
  waiting for transfers between devices  78.8 us (39%)
  blocking collectives  77.8 us (38%)
  between operations  14.5 us (7%)
  matrix products  11.3 us (6%)
  other arithmetic  10.8 us (5%)
  local copies, waits for them, and re-layouts  9.03 us (4%)
    all_gather x1, waiting for transfers between devices, shards(): full_x = lax.all_gather(embeddings, 'cls', axis=1, tiled=True)  61.6 us
    pmax x2, blocking collectives, shards(): top = lax.pmax(local_top, 'cls')  40.6 us
    psum x2, blocking collectives, shards(): lax.psum((jnp.sum(jnp.exp(logits - top[:, None]), axis=1), label_term), '...  34.6 us
    all_gather x2, waiting for transfers between devices, shards(): grad = jnp.sum(lax.all_gather(grad_local, 'img'), axis=0)  16.5 us
    dot_general x2, matrix products, shards(): lax.dot_general(full_x, resid, (((0,), (0,)), ((), ())), preferred_elemen...  6.25 us
    all_gather x2, local copies, waits for them, and re-layouts, shards(): grad = jnp.sum(lax.all_gather(grad_local, 'img'), axis=0)  6.07 us
    reduce_sum x2, other arithmetic, shards(): grad = jnp.sum(lax.all_gather(grad_local, 'img'), axis=0)  6.02 us
    dot_general x2, matrix products, shards(): jnp.dot(full_x, operand, preferred_element_type=jnp.float32) * scale  5.04 us
  transfers between devices with their start and end apart: 3, of which 3 were waited for; matrix products, arithmetic and copies ran while one was open for 1% of the time, Pallas kernels for 0%

profile of v1, /device:TPU:0, one launch (start us, length us, event | category | flops | bytes accessed | tf_op | source)
XLA Modules:
  0.0 202.4 jit_solution(1376812383107186998)
XLA Ops:
  7.2 0.0 all-gather.6.cloned.1.call-start
  7.2 0.7 all-gather.6.cloned.1.call-update
  7.9 0.0 all-gather.8.cloned.1.call-start
  7.9 1.2 copy.6
  9.1 0.0 copy-start.3
  9.1 2.6 %all_gather.18 = f32[1536,128]{0,1:T(8,128)} all-gather(f32[768,128]{0,1:T(8,128)S(1)} %copy.6), channel_id=1, replica_groups=mesh['grp'=2,'cls'=8,'img'=2] {'img'}, dimensions={0}, use_global_device_ids=true | all-gather | bytes 1179648 | tf_op jit(solution)/shard_map/all_gather | solution.py:24
  11.7 61.6 %all-gather.6.cloned.1.call-done = bf16[1024,1536]{0,1:T(8,128)(2,1)} async-done(((bf16[1024,192]{0,1:T(8,128)(2,1)}), bf16[1024,1536]{0,1:T(8,128)(2,1)}) %all-gather.6.cloned.1.call-update) | async-done | bytes 3145744 | tf_op jit(solution)/shard_map/all_gather | solution.py:19
  73.4 0.0 copy-start
  73.4 3.7 %fusion.19 = (f32[1024]{0:T(1024)S(1)}, f32[1024,128]{0,1:T(8,128)}) fusion(bf16[1024,1536]{0,1:T(8,128)(2,1)} %all-gather.6.cloned.1.call-done, f32[1536,128]{0,1:T(8,128)} %all_gather.18), kind=kOutput, calls=%fused_computation.34 | convolution fusion | flops 403110912 | bytes 4460544 | tf_op jit(solution)/shard_map/dot_general | solution.py:28
  77.0 19.0 %pmax.14 = f32[1024]{0:T(1024)S(1)} all-reduce(f32[1024]{0:T(1024)S(1)} %get-tuple-element.10), channel_id=1, replica_groups=mesh['grp'=2,'cls'=8,'img'=2] {'cls'}, use_global_device_ids=true, to_apply=%region_1.0 | all-reduce | flops 1024 | bytes 8192 | tf_op jit(solution)/shard_map/pmax | solution.py:31
  96.1 1.1 exponential_reduce_fusion
  97.2 17.2 %psum.21 = f32[1024]{0:T(1024)S(1)} all-reduce(f32[1024]{0:T(1024)S(1)} %exponential_reduce_fusion), channel_id=1, replica_groups=mesh['grp'=2,'cls'=8,'img'=2] {'cls'}, use_global_device_ids=true, to_apply=%region_3.0 | all-reduce | flops 1024 | bytes 8192 | tf_op jit(solution)/shard_map/psum | solution.py:32
  114.4 0.0 copy-done.3
  114.4 0.0 copy-done
  114.4 3.1 %fusion = f32[1536,128]{0,1:T(8,128)} fusion(bf16[1024,1536]{0,1:T(8,128)(2,1)S(1)} %copy-done, f32[1024,128]{0,1:T(8,128)} %get-tuple-element.11, s32[1024]{0:T(1024)S(1)} %copy-done.3, f32[1024]{0:T(1024)S(1)} %log_add_fusion.1, s32[128]{0:T(128)S(1)} %iota_add_fusion), kind=kOutput, calls=%fused_computation.2 | convolution fusion | flops 403505152 | bytes 4465152 | tf_op jit(solution)/shard_map/dot_general | solution.py:39
  117.6 0.0 all-gather.8.cloned.1.call-update
  117.6 0.0 all-gather.10.cloned.1.call-start
  118.3 7.8 %all-gather.8.cloned.1.call-done = f32[3072,128]{0,1:T(8,128)} async-done(((f32[1536,128]{0,1:T(8,128)}), f32[3072,128]{0,1:T(8,128)}) %all-gather.8.cloned.1.call-update) | async-done | bytes 1572880 | tf_op jit(solution)/shard_map/all_gather | solution.py:44
  126.1 3.4 %reshape.19 = f32[2,1536,128]{1,0,2:T(2,128)} reshape(f32[3072,128]{0,1:T(8,128)} %all-gather.8.cloned.1.call-done) | data formatting | bytes 3145728 | tf_op jit(solution)/shard_map/all_gather | solution.py:44
  129.6 4.2 %reduce_sum.46 = f32[1536,128]{0,1:T(8,128)} reduce(f32[2,1536,128]{1,0,2:T(2,128)} %reshape.19, f32[]{:T(128)} %constant.14.clone.1), dimensions={0}, to_apply=%region_4.0 | reduce | flops 196608 | bytes 2359300 | tf_op jit(solution)/shard_map/reduce_sum | solution.py:44
  133.7 1.7 maximum_multiply_fusion
  135.4 0.0 copy-start.1
  135.4 0.9 copy-done.1
  136.3 1.4 fusion.20
  137.7 21.6 %pmax.15 = f32[1024]{0:T(1024)S(1)} all-reduce(f32[1024]{0:T(1024)S(1)} %get-tuple-element.12), channel_id=1, replica_groups=mesh['grp'=2,'cls'=8,'img'=2] {'cls'}, use_global_device_ids=true, to_apply=%region_6.0 | all-reduce | flops 1024 | bytes 8192 | tf_op jit(solution)/shard_map/pmax | solution.py:31
  159.3 1.2 fusion.2
  160.5 17.4 %all-reduce = (f32[1024]{0:T(1024)S(1)}, f32[1024]{0:T(1024)S(1)}) all-reduce(f32[1024]{0:T(1024)S(1)} %get-tuple-element.5, f32[1024]{0:T(1024)S(1)} %get-tuple-element.4), channel_id=1, replica_groups=mesh['grp'=2,'cls'=8,'img'=2] {'cls'}, use_global_device_ids=true, to_apply=%region_8.0 | all-reduce | flops 2048 | bytes 16384 | tf_op jit(solution)/shard_map/psum | solution.py:32
  177.9 0.6 fusion.18
  178.5 3.1 %fusion.1 = f32[1536,128]{0,1:T(8,128)} fusion(bf16[1024,1536]{0,1:T(8,128)(2,1)S(1)} %copy-done, f32[128,1024]{1,0:T(8,128)} %get-tuple-element.13, f32[1024]{0:T(1024)S(1)} %get-tuple-element.9, s32[1024]{0:T(1024)S(1)} %copy-done.3, s32[128]{0:T(128)S(1)} %iota_add_fusion), kind=kOutput, calls=%fused_computation.3 | convolution fusion | flops 403505152 | bytes 4465152 | tf_op jit(solution)/shard_map/dot_general | solution.py:39
  181.6 0.0 copy-start.2
  181.6 0.0 all-gather.10.cloned.1.call-update
  181.6 8.6 %all-gather.10.cloned.1.call-done = f32[3072,128]{0,1:T(8,128)} async-done(((f32[1536,128]{0,1:T(8,128)}), f32[3072,128]{0,1:T(8,128)}) %all-gather.10.cloned.1.call-update) | async-done | bytes 1572880 | tf_op jit(solution)/shard_map/all_gather | solution.py:44
  190.3 2.6 %reshape.20 = f32[2,1536,128]{1,0,2:T(2,128)S(1)} reshape(f32[3072,128]{0,1:T(8,128)} %all-gather.10.cloned.1.call-done) | data formatting | bytes 3145728 | tf_op jit(solution)/shard_map/all_gather | solution.py:44
  192.9 1.9 reduce_sum.48
  194.8 0.0 copy-done.2
  194.8 0.2 maximum_multiply_fusion.1
  195.0 0.9 copy.7
  (2 shorter events, 0.0 us)
Async XLA Ops:
  7.2 66.2 %all-gather.6.cloned.1.call-start = ((), (), s32[]{:S(2)}) async-start(), calls=%async_computation | async-start | bytes 3538944 | tf_op jit(solution)/shard_map/all_gather | solution.py:19
  7.9 118.2 %all-gather.8.cloned.1.call-start = ((), (), s32[]{:S(2)}) async-start(), calls=%async_computation.1 | async-start | bytes 2359296 | tf_op jit(solution)/shard_map/all_gather | solution.py:44
  9.1 105.3 %copy-start.3 = (s32[1024]{0:T(1024)S(1)}, s32[1024]{0:T(1024)}, u32[]{:S(2)}) copy-start(s32[1024]{0:T(1024)} %param.5) | copy-start | bytes 12292
  73.4 41.1 %copy-start = (bf16[1024,1536]{0,1:T(8,128)(2,1)S(1)}, bf16[1024,1536]{0,1:T(8,128)(2,1)}, u32[]{:S(2)}) copy-start(bf16[1024,1536]{0,1:T(8,128)(2,1)} %all-gather.6.cloned.1.call-done) | copy-start | bytes 9437188
  117.6 72.7 %all-gather.10.cloned.1.call-start = ((), (), s32[]{:S(2)}) async-start(), calls=%async_computation.2 | async-start | bytes 2359296 | tf_op jit(solution)/shard_map/all_gather | solution.py:44
  135.4 0.9 copy-start.1
  181.6 13.2 %copy-start.2 = (f32[1536,128]{0,1:T(8,128)S(1)}, f32[1536,128]{0,1:T(8,128)}, u32[]{:S(2)}) copy-start(f32[1536,128]{0,1:T(8,128)} %copy-done.1) | copy-start | bytes 2359300
Sparse Core Ops, SparseCore 0:
  10.2 63.1 all-gather.5
  117.7 8.3 all-gather.7
  181.8 8.4 all-gather.9
